TPU v7x, 32 devices: a whole 2x2x4 slice. The times are simulated.
32 devices in a mesh: dir: 2 (over y), row: 4 (over z), col: 4 (over x, core).
Axes of the slice: x: 2, y: 2, z: 4, core: 2. Of those that a mesh axis runs over, the one named last changes fastest.
Arguments:
- cotangent: bfloat16 [2048, 512], P('dir'), may hold values from -3 to 3
- radiation: bfloat16 [2, 8192, 2048], P(None, ('row', 'col'), 'dir'), may hold values from -0.125 to 0.125
- near_z: float32 [2, 256, 512, 512], P(None, ('dir', 'row', 'col')), may hold values from -0.25 to 0.25
- near_pairs: int32 [256, 2], P(('dir', 'row', 'col')), may hold values from 0 to 15, as said below
- far_ut: float32 [2, 128, 96, 512], P(None, ('dir', 'row', 'col')), may hold values from -0.25 to 0.25
- far_vt: float32 [2, 128, 96, 512], P(None, ('dir', 'row', 'col')), may hold values from -0.625 to 0.625
- far_pairs: int32 [128, 2], P(('dir', 'row', 'col')), may hold values from 0 to 15, as said below
- far_ranks: int32 [128], P(('dir', 'row', 'col')), may hold values from 32 to 96
- block_counts: int32 [32, 2], P(('dir', 'row', 'col')), may hold values from 1 to 8, as said below
Outputs:
- adjoint: float32 [8192, 512], P(('col', 'dir', 'row'))
Inputs may be any that keep to these rules, and one draw needn't show every extreme that they name: `near_pairs`: slot s belongs to the device at position g = s div 8 in the order dir, row, col, with row index r and column index c; its row cluster lies in r * 4 to (r + 1) * 4 - 1 and its column cluster in c * 4 to (c + 1) * 4 - 1. Pairs may repeat. `far_pairs`: slot s belongs to the device at position s div 4 in the order dir, row, col, with row index r and column index c; its row cluster lies in r * 4 to (r + 1) * 4 - 1 and its column cluster in c * 4 to (c + 1) * 4 - 1. Pairs may repeat. `block_counts`: column 0 is at most 8 and column 1 at most 4; the live slots of a device are its first ones.
All inputs are finite; a program needn't handle non-finite values.
Results may differ from a plain program's by a relative error of at most 0.0003.
Values sent between devices are 32-bit elements; how exact they have to be, the bound alone decides.
A program may use at most 128 MiB of HBM per device.

v0:
```python
import jax
import jax.numpy as jnp
from jax import lax
from jax.sharding import PartitionSpec as P


def swap_parts(values):
    half_width = values.shape[1] // 2
    return jnp.concatenate([-values[:, half_width:], values[:, :half_width]], axis=1)


def transposed_dot(left, right):
    return lax.dot_general(
        left,
        right,
        (((0,), (0,)), ((), ())),
        precision=lax.Precision.HIGHEST,
        preferred_element_type=jnp.float32,
    )


def plain_dot(left, right):
    return jnp.dot(left, right, precision=lax.Precision.HIGHEST, preferred_element_type=jnp.float32)


def add_rows(total, term, start):
    current = lax.dynamic_slice_in_dim(total, start, term.shape[0], 0)
    return lax.dynamic_update_slice_in_dim(total, current + term, start, 0)


def shards(
    cotangent, radiation, near_z, near_pairs, far_ut, far_vt, far_pairs, far_ranks, block_counts
):
    block_rows = near_z.shape[2]
    rank_most = far_ut.shape[2]
    partial_rhs = jnp.dot(radiation[0], cotangent, preferred_element_type=jnp.float32) + jnp.dot(
        radiation[1], swap_parts(cotangent), preferred_element_type=jnp.float32
    )
    summed = lax.psum(partial_rhs, "dir")
    shard_rhs = lax.all_gather(summed, "col", axis=0, tiled=True)
    swapped_rhs = swap_parts(shard_rhs)
    row_base = lax.axis_index("row") * lax.axis_size("col")
    col_base = lax.axis_index("col") * lax.axis_size("row")
    column_rows = lax.axis_size("row") * block_rows

    def near_step(slot_index, total):
        row_start = (near_pairs[slot_index, 0] - row_base) * block_rows
        col_start = (near_pairs[slot_index, 1] - col_base) * block_rows
        source = lax.dynamic_slice_in_dim(shard_rhs, row_start, block_rows, 0)
        source_swap = lax.dynamic_slice_in_dim(swapped_rhs, row_start, block_rows, 0)
        blocks = near_z[:, slot_index]
        term = transposed_dot(blocks[0], source) + transposed_dot(blocks[1], source_swap)
        return add_rows(total, term, col_start)

    def far_step(slot_index, total):
        row_start = (far_pairs[slot_index, 0] - row_base) * block_rows
        col_start = (far_pairs[slot_index, 1] - col_base) * block_rows
        source = lax.dynamic_slice_in_dim(shard_rhs, row_start, block_rows, 0)
        source_swap = lax.dynamic_slice_in_dim(swapped_rhs, row_start, block_rows, 0)
        left_f = far_ut[:, slot_index]
        right_f = far_vt[:, slot_index]
        coeffs = plain_dot(left_f[0], source) + plain_dot(left_f[1], source_swap)
        keep_rows = (lax.iota(jnp.int32, rank_most) < far_ranks[slot_index])[:, None]
        coeffs = jnp.where(keep_rows, coeffs, jnp.zeros_like(coeffs))
        term = transposed_dot(right_f[0], coeffs) + transposed_dot(right_f[1], swap_parts(coeffs))
        return add_rows(total, term, col_start)

    partial_out = jnp.zeros((column_rows, shard_rhs.shape[1]), jnp.float32)
    partial_out = lax.fori_loop(0, block_counts[0, 0], near_step, partial_out)
    partial_out = lax.fori_loop(0, block_counts[0, 1], far_step, partial_out)
    result = lax.psum_scatter(partial_out, ("dir", "row"), scatter_dimension=0, tiled=True)
    return result


def solution(mesh):
    return jax.shard_map(
        shards,
        mesh=mesh,
        in_specs=(
            P("dir", None),
            P(None, ("row", "col"), "dir"),
            P(None, ("dir", "row", "col"), None, None),
            P(("dir", "row", "col"), None),
            P(None, ("dir", "row", "col"), None, None),
            P(None, ("dir", "row", "col"), None, None),
            P(("dir", "row", "col"), None),
            P(("dir", "row", "col")),
            P(("dir", "row", "col"), None),
        ),
        out_specs=P(("col", "dir", "row"), None),
        check_vma=False,
    )
```

profile of v0, /device:TPU:0, one launch (start us, length us, event | category | flops | bytes accessed | tf_op | source)
XLA Modules:
  0.0 334.3 jit_solution(14046022511237606327)
XLA Ops:
  6.5 1.4 slice_negate_fusion.2
  8.0 2.2 fusion.27
  10.2 0.0 copy-start.2
  10.2 0.0 copy-done.3
  10.2 1.7 fusion.22
  11.9 0.0 all-reduce.2.cloned.1.call-update
  12.0 0.0 all-gather.2.cloned.1.call-start
  12.0 42.9 %all-reduce.2.cloned.1.call-done = f32[512,512]{1,0:T(8,128)} async-done(((f32[512,512]{1,0:T(8,128)}), f32[512,512]{1,0:T(8,128)}) %all-reduce.2.cloned.1.call-update) | async-done | bytes 1048592 | tf_op jit(solution)/shard_map/psum | solution.py:39
  54.9 0.0 all-gather.2.cloned.1.call-update
  55.0 0.0 reduce-scatter.2.cloned.1.call-start
  55.0 0.6 fusion.32
  55.7 35.3 %all-gather.2.cloned.1.call-done = f32[2048,512]{1,0:T(8,128)} async-done(((f32[512,512]{1,0:T(8,128)}), f32[2048,512]{1,0:T(8,128)}) %all-gather.2.cloned.1.call-update) | async-done | bytes 4194320 | tf_op jit(solution)/shard_map/all_gather | solution.py:40
  91.0 2.5 slice_negate_fusion.1
  93.5 2.5 pad_maximum_fusion
  96.0 2.5 broadcast_in_dim.12
  98.5 22.3 %while.20 = (s32[]{:T(128)}, f32[2048,512]{1,0:T(8,128)}, s32[]{:T(128)}, s32[8,2]{0,1:T(2,128)S(1)}, s32[]{:T(128)}, /*index=5*/f32[2,8,512,512]{3,2,1,0:T(8,12...) while((s32[]{:T(128)}, f32[2048,512]{1,0:T(8,128)}, ...), condition=%wide.region_2.0_spmd, body=%wide.region_1.0_spmd.sunk | while | flops 3221749760 | bytes 8388963 | solution.py:69
  99.2 0.6 constant_dynamic-slice_fusion.6
  101.1 3.4 %fusion.49 = f32[512,512]{1,0:T(8,128)S(1)} fusion(f32[2,8,512,512]{3,2,1,0:T(8,128)} %get-tuple-element.336, s32[]{:T(128)S(6)} %select_n.40, f32[2048,512]{1,0:T(8,128)} %get-tuple-element.338, s32[]{:T(128)S(6)} %select_n.42), kind=kOutput, calls=%fused_computation.5.clone.1 | convolution fusion | flops 1610612736 | bytes 3145736 | tf_op jit(solution)/shard_map/while/body/dot_general | solution.py:13
  104.5 4.8 %fusion.50 = f32[2048,512]{1,0:T(8,128)} fusion(f32[2048,512]{1,0:T(8,128)} %get-tuple-element.317, s32[]{:T(128)S(6)} %select_n.41, f32[512,512]{1,0:T(8,128)S(1)} %fusion.49, f32[2,8,512,512]{3,2,1,0:T(8,128)} %get-tuple-element.336, s32[]{:T(128)S(6)} %add.101, s32[]{:T(128)S(6)} %select_n.40, f32[2048,512]{1,0:T(8,128)} %get-tuple-element.339, ...), kind=kOutput, calls=%fused_computation.2.clone.1 | convolution fusion | flops 1611137024 | bytes 5242896 | tf_op jit(solution)/shard_map/while/body/dot_general | solution.py:13
  110.0 0.6 constant_dynamic-slice_fusion.6
  111.9 3.4 %fusion.49 = f32[512,512]{1,0:T(8,128)S(1)} fusion(f32[2,8,512,512]{3,2,1,0:T(8,128)} %get-tuple-element.336, s32[]{:T(128)S(6)} %select_n.40, f32[2048,512]{1,0:T(8,128)} %get-tuple-element.338, s32[]{:T(128)S(6)} %select_n.42), kind=kOutput, calls=%fused_computation.5.clone.1 | convolution fusion | flops 1610612736 | bytes 3145736 | tf_op jit(solution)/shard_map/while/body/dot_general | solution.py:13
  115.3 4.8 %fusion.50 = f32[2048,512]{1,0:T(8,128)} fusion(f32[2048,512]{1,0:T(8,128)} %get-tuple-element.317, s32[]{:T(128)S(6)} %select_n.41, f32[512,512]{1,0:T(8,128)S(1)} %fusion.49, f32[2,8,512,512]{3,2,1,0:T(8,128)} %get-tuple-element.336, s32[]{:T(128)S(6)} %add.101, s32[]{:T(128)S(6)} %select_n.40, f32[2048,512]{1,0:T(8,128)} %get-tuple-element.339, ...), kind=kOutput, calls=%fused_computation.2.clone.1 | convolution fusion | flops 1611137024 | bytes 5242896 | tf_op jit(solution)/shard_map/while/body/dot_general | solution.py:13
  120.8 14.2 %while.21 = (s32[]{:T(128)}, f32[2048,512]{1,0:T(8,128)}, s32[]{:T(128)}, s32[4,2]{0,1:T(2,128)S(1)}, s32[]{:T(128)}, /*index=5*/f32[2,4,96,512]{3,2,1,0:T(8,128...) while((s32[]{:T(128)}, f32[2048,512]{1,0:T(8,128)}, ...), condition=%wide.region_4.5_spmd, body=%wide.region_3.4_spmd.sunk | while | flops 1208656000 | bytes 8454735 | solution.py:70
  121.4 0.7 dynamic_slice.73
  122.1 0.7 iota_compare_fusion.2
  122.8 0.7 constant_dynamic-slice_fusion.7
  124.7 2.1 fusion.55
  126.8 2.1 fusion.56
  128.9 2.0 fusion.57
  130.9 3.5 %fusion.58 = f32[2048,512]{1,0:T(8,128)} fusion(f32[2048,512]{1,0:T(8,128)} %get-tuple-element.364, s32[]{:T(128)S(6)} %select_n.45, f32[512,512]{1,0:T(8,128)S(1)} %fusion.57, f32[2,4,96,512]{3,2,1,0:T(8,128)} %get-tuple-element.385, s32[]{:T(128)S(6)} %add.109, s32[]{:T(128)S(6)} %select_n.44, f32[96,256]{1,0:T(8,128)S(1)} %get-tuple-element.299, ...), kind=kOutput, calls=%fused_computation.14.clone.1 | convolution fusion | flops 302563328 | bytes 3538956 | tf_op jit(solution)/shard_map/while/body/dot_general | solution.py:13
  135.0 0.0 reduce-scatter.2.cloned.1.call-update
  135.0 192.8 %reduce-scatter.2.cloned.1.call-done = f32[256,512]{1,0:T(8,128)} async-done(((f32[2048,512]{1,0:T(8,128)}), f32[256,512]{1,0:T(8,128)}) %reduce-scatter.2.cloned.1.call-update) | async-done | bytes 524304 | tf_op jit(solution)/shard_map/reduce_scatter | solution.py:71
  (10 shorter events, 0.0 us)
Async XLA Ops:
  6.5 3.7 %copy-start.3 = (bf16[2,512,1024]{2,1,0:T(8,128)(2,1)S(1)}, bf16[2,512,1024]{2,1,0:T(8,128)(2,1)}, u32[]{:S(2)}) copy-start(bf16[2,512,1024]{2,1,0:T(8,128)(2,1)} %param.14) | copy-start | bytes 6291460
  6.5 48.4 %all-reduce.2.cloned.1.call-start = ((), (), s32[]{:S(2)}) async-start(), calls=%async_computation.1 | async-start | bytes 2097152 | tf_op jit(solution)/shard_map/psum | solution.py:39
  10.2 44.8 %copy-start.2 = (s32[1,2]{1,0:T(1,128)S(1)}, s32[1,2]{1,0:T(1,128)}, u32[]{:S(2)}) copy-start(s32[1,2]{1,0:T(1,128)} %param.21) | copy-start | bytes 28
  12.0 79.0 %all-gather.2.cloned.1.call-start = ((), (), s32[]{:S(2)}) async-start(), calls=%async_computation.2 | async-start | bytes 5242880 | tf_op jit(solution)/shard_map/all_gather | solution.py:40
  55.0 272.9 %reduce-scatter.2.cloned.1.call-start = ((), (), s32[]{:S(2)}) async-start(), calls=%async_computation.3 | async-start | bytes 4718592 | tf_op jit(solution)/shard_map/reduce_scatter | solution.py:71
  96.0 2.5 copy-start
  98.5 22.3 %copy-start.1 = (s32[4,2]{0,1:T(2,128)S(1)}, s32[4,2]{0,1:T(2,128)}, u32[]{:S(2)}) copy-start(s32[4,2]{0,1:T(2,128)} %param.19) | copy-start | bytes 100
  98.5 22.3 %copy-start.4 = (s32[4]{0:T(128)S(1)}, s32[4]{0:T(128)}, u32[]{:S(2)}) copy-start(s32[4]{0:T(128)} %param.20) | copy-start | bytes 52
Sparse Core Ops, SparseCore 0:
  12.1 42.8 all-reduce.1
  56.5 34.4 all-gather.1
  135.1 192.6 reduce-scatter.1
where the time goes:
time: 335 us; the launch traced here: 334 us
  waiting for transfers between devices  271 us (81%)
  matrix products  29.9 us (9%)
  between operations  13.2 us (4%)
  loops' own time  7.19 us (2%)
  other arithmetic  7.13 us (2%)
  local copies, waits for them, and re-layouts  5.73 us (2%)
    reduce_scatter x1, waiting for transfers between devices, shards(): lax.psum_scatter(partial_out, ('dir', 'row'), scatter_dimension=0, tiled=...  193 us
    psum x1, waiting for transfers between devices, shards(): summed = lax.psum(partial_rhs, 'dir')  42.9 us
    all_gather x1, waiting for transfers between devices, shards(): shard_rhs = lax.all_gather(summed, 'col', axis=0, tiled=True)  35.3 us
    dot_general x6, matrix products, transposed_dot(): lax.dot_general(left, right, (((0,), (0,)), ((), ())), precision=lax.Prec...  21.8 us
  transfers between devices with their start and end apart: 3, of which 3 were waited for; matrix products, arithmetic and copies ran while one was open for 0% of the time, Pallas kernels for 0%

commit v1 on v0

v1 whole, which is shorter than its diff:
```python
import functools

import jax
import jax.numpy as jnp
from jax import lax
from jax.experimental import pallas as pl
from jax.experimental.pallas import tpu as pltpu
from jax.sharding import PartitionSpec as P

CHUNKS = 4
CORES = 2
MESH = pl.DeviceIdType.MESH
F32 = jnp.float32
BF16 = jnp.bfloat16
NT = (((1,), (1,)), ((), ()))


def dot(left, right):
    return jnp.dot(left, right, preferred_element_type=F32)


def dot_nt(left, right):
    return lax.dot_general(left, right, NT, preferred_element_type=F32)


def split(values):
    high = values.astype(BF16)
    return high, (values - high.astype(F32)).astype(BF16)


def swap_rows(values):
    half = values.shape[0] // 2
    return jnp.concatenate([-values[half:], values[:half]], axis=0)


def fold(values):
    half = values.shape[0] // 2
    return values[:half] + values[half:]


def kernel(
    n_dir, n_row, n_col, depth,
    near_pairs, far_pairs, far_ranks, counts, cot, rad, near_z, far_ut, far_vt,
    out,
    z_high, z_low, stage, ut, vt, sent, dir_in, gathered, sides, terms, parts, dir_parts, sums, row_parts,
    stage_sem, far_sem, d_send, d_recv, x_send, x_recv, c_send, c_recv, p_send, p_recv, r_send, r_recv,
):
    chunks, width = cot.shape[0], cot.shape[1]
    n_near, n_far = near_z.shape[1], far_ut.shape[1]
    block = near_z.shape[2]
    piece = block // n_dir
    n_x = n_col // CORES
    per_dir = n_row // n_dir
    d = lax.axis_index("dir")
    r = lax.axis_index("row")
    c = lax.axis_index("col")
    x, core = c // CORES, c % CORES
    partner = x * CORES + (CORES - 1 - core)

    def dir_peer(j):
        return (lax.rem(d + j, n_dir), r, c)

    def x_peer(j):
        return (d, r, lax.rem(x + j, n_x) * CORES + core)

    def row_peer(i):
        return (d, lax.rem(r + i, n_row), c)

    def from_x(j, core_of):
        return lax.rem(x + n_x - j, n_x) * CORES + core_of

    def remote(src, dst, send, recv, device):
        return pltpu.make_async_remote_copy(
            src_ref=src, dst_ref=dst, send_sem=send, recv_sem=recv, device_id=device, device_id_type=MESH
        )

    def load_item(item):
        slot, part = item // 2, lax.rem(item, 2)
        return pltpu.make_async_copy(
            near_z.at[part, slot], stage.at[lax.rem(item, 2)], stage_sem.at[lax.rem(item, 2)]
        )

    load_item(0).start()
    load_item(1).start()
    far_loads = [
        pltpu.make_async_copy(far_ut, ut, far_sem.at[0]),
        pltpu.make_async_copy(far_vt, vt, far_sem.at[1]),
    ]
    for load in far_loads:
        load.start()

    peers = [dir_peer(j) for j in range(1, n_dir)]
    peers += [x_peer(j) for j in range(1, n_x)]
    peers += [row_peer(i) for i in range(1, n_row)]
    peers.append((d, r, partner))
    barrier = pltpu.get_barrier_semaphore()
    for device in peers:
        pl.semaphore_signal(barrier, inc=1, device_id=device, device_id_type=MESH)
    pl.semaphore_wait(barrier, len(peers))

    def send_dir(k, j):
        return remote(sent.at[k], dir_in.at[k, j - 1], d_send.at[k, j - 1], d_recv.at[k, j - 1], dir_peer(j))

    def send_x(k, j):
        return remote(gathered.at[k, c], gathered.at[k, c], x_send.at[k, j - 1], x_recv.at[k, j - 1], x_peer(j))

    def send_core(k, j, core_of):
        which = from_x(j, core_of)
        return remote(
            gathered.at[k, which], gathered.at[k, which], c_send.at[k, j], c_recv.at[k, j], (d, r, partner)
        )

    def send_part(k, j, q):
        owner = lax.rem(d + j, n_dir)
        return remote(
            parts.at[k % depth, owner * n_row + q],
            dir_parts.at[k, j - 1, q],
            p_send.at[k, j - 1, q],
            p_recv.at[k, j - 1, q],
            dir_peer(j),
        )

    def send_row(k, q):
        return remote(
            sums.at[k, q], row_parts.at[k, r], r_send.at[k, q], r_recv.at[k, r], (d, q, c)
        )

    def right_sides(k):
        left = cot[k]
        sent[k] = dot_nt(left, rad[0]) + dot_nt(swap_rows(left), rad[1])
        for j in range(1, n_dir):
            send_dir(k, j).start()

    def convert(first, last):
        def body(item, carry):
            load_item(item).wait()
            high, low = split(stage[lax.rem(item, 2)])
            rows = pl.ds(pl.multiple_of(lax.rem(item, 2) * block, block), block)
            z_high[item // 2, rows, :] = high
            z_low[item // 2, rows, :] = low

            @pl.when(item + 2 < 2 * n_near)
            def _():
                load_item(item + 2).start()

            return carry

        lax.fori_loop(2 * first, 2 * last, body, 0)

    def add_dirs(k):
        for j in range(1, n_dir):
            send_dir(k, j).wait_recv()
        total = sent[k]
        for j in range(1, n_dir):
            total = total + dir_in[k, j - 1]
        gathered[k, c] = total
        for j in range(1, n_x):
            send_x(k, j).start()
        send_core(k, 0, core).start()

    def relay(k):
        for j in range(1, n_x):
            which = from_x(j, core)
            remote(
                gathered.at[k, which], gathered.at[k, which], x_send.at[k, j - 1], x_recv.at[k, j - 1], x_peer(j)
            ).wait_recv()
            send_core(k, j, core).start()

    def products(k):
        for j in range(n_x):
            send_core(k, j, CORES - 1 - core).wait_recv()

        def side(q, carry):
            values = gathered[k, q]
            high, low = split(jnp.concatenate([values, swap_rows(values)], axis=1))
            sides[q, :width] = high
            sides[q, width:] = low
            return carry

        lax.fori_loop(0, n_col, side, 0)

        def near(s, carry):
            left = sides[lax.rem(near_pairs[s, 0], n_col)]
            terms[s] = fold(dot(left, z_high[s])) + dot(left[:width], z_low[s])
            return carry

        lax.fori_loop(0, n_near, near, 0)

        def far(s, carry):
            left = sides[lax.rem(far_pairs[s, 0], n_col)]
            high, low = split(jnp.concatenate([ut[0, s], ut[1, s]], axis=1))
            coeffs = fold(dot_nt(left, high)) + dot_nt(left[:width], low)
            lanes = lax.broadcasted_iota(jnp.int32, coeffs.shape, 1)
            coeffs = jnp.where(lanes < far_ranks[s], coeffs, 0.0)
            c_high, c_low = split(coeffs)
            s_high, s_low = split(swap_rows(coeffs))
            re_high, re_low = split(vt[0, s])
            im_high, im_low = split(vt[1, s])
            both = dot(jnp.concatenate([c_high, c_low], axis=0), re_high)
            both = both + dot(jnp.concatenate([s_high, s_low], axis=0), im_high)
            terms[n_near + s] = fold(both) + (dot(c_high, re_low) + dot(s_high, im_low))
            return carry

        lax.fori_loop(0, n_far, far, 0)

        if k >= depth:
            for j in range(1, n_dir):
                for q in range(n_row):
                    send_part(k - depth, j, q).wait_send()
        for t in range(n_row):
            j, q0 = 1 + t // per_dir, (t % per_dir) * n_dir
            cluster = lax.rem(lax.rem(d + j, n_dir) * per_dir + t % per_dir, n_row)
            target = c * n_row + cluster
            gains = [
                jnp.where((near_pairs[s, 1] == target) & (s < counts[0, 0]), 1.0, 0.0) for s in range(n_near)
            ] + [
                jnp.where((far_pairs[s, 1] == target) & (s < counts[0, 1]), 1.0, 0.0) for s in range(n_far)
            ]
            for h in range(n_dir):
                lanes = slice(h * piece, (h + 1) * piece)
                total = terms[0, :, lanes] * gains[0]
                for s in range(1, n_near + n_far):
                    total = total + terms[s, :, lanes] * gains[s]
                parts[k % depth, cluster * n_dir + h] = total
                if j < n_dir:
                    send_part(k, j, q0 + h).start()
        for q in range(n_row):
            sums[k, q] = parts[k % depth, d * n_row + q]

    def add_parts(k):
        for q in range(n_row):
            for j in range(1, n_dir):
                send_part(k, j, q).wait_recv()
                sums[k, q] = sums[k, q] + dir_parts[k, j - 1, q]

            @pl.when(q != r)
            def _():
                send_row(k, q).start()

    def finish(k):
        total = sums[k, r]
        for i in range(1, n_row):
            src = lax.rem(r + i, n_row)
            remote(
                sums.at[k, src], row_parts.at[k, src], r_send.at[k, src], r_recv.at[k, src], row_peer(i)
            ).wait_recv()
            total = total + row_parts[k, src]
        out[k] = total

    for k in range(chunks):
        right_sides(k)
    steps = chunks
    edges = [n_near * i // steps for i in range(steps + 1)]
    for i in range(steps):
        convert(edges[i], edges[i + 1])
        if i < chunks - 1:
            add_dirs(i)
        if i >= 1:
            relay(i - 1)
    for load in far_loads:
        load.wait()
    products(0)
    add_dirs(chunks - 1)
    for k in range(1, chunks):
        products(k) if k < chunks - 1 else None
        if k == 1:
            relay(chunks - 1)
        if k == chunks - 1:
            add_parts(0)
            products(k)
    for k in range(1, chunks):
        add_parts(k)
        finish(k - 1)
    finish(chunks - 1)

    for k in range(chunks):
        for j in range(1, n_dir):
            send_dir(k, j).wait_send()
            if k >= chunks - depth:
                for q in range(n_row):
                    send_part(k, j, q).wait_send()
        for j in range(1, n_x):
            send_x(k, j).wait_send()
        for j in range(n_x):
            send_core(k, j, core).wait_send()
        for q in range(n_row):

            @pl.when(q != r)
            def _():
                send_row(k, q).wait_send()


def shards(
    cotangent, radiation, near_z, near_pairs, far_ut, far_vt, far_pairs, far_ranks, block_counts
):
    n_dir, n_row, n_col = (lax.axis_size(name) for name in ("dir", "row", "col"))
    deep, wide = cotangent.shape
    chunks, width = CHUNKS, wide // CHUNKS
    block = near_z.shape[2]
    n_near, n_far, rank_most = near_z.shape[1], far_ut.shape[1], far_ut.shape[2]
    n_x = n_col // CORES
    piece = block // n_dir
    depth = chunks if n_row * n_col <= 16 else 2
    cot = cotangent.T.reshape(2, chunks, width // 2, deep).transpose(1, 0, 2, 3).reshape(chunks, width, deep)
    vmem = pl.BlockSpec(memory_space=pltpu.VMEM)
    smem = pl.BlockSpec(memory_space=pltpu.SMEM)
    anywhere = pl.BlockSpec(memory_space=pl.ANY)
    dma = pltpu.SemaphoreType.DMA
    result = pl.pallas_call(
        functools.partial(kernel, n_dir, n_row, n_col, depth),
        out_shape=jax.ShapeDtypeStruct((chunks, width, piece), F32),
        in_specs=[smem] * 4 + [vmem] * 2 + [anywhere] * 3,
        out_specs=vmem,
        scratch_shapes=[
            pltpu.VMEM((n_near, 2 * block, block), BF16),
            pltpu.VMEM((n_near, 2 * block, block), BF16),
            pltpu.VMEM((2, block, block), F32),
            pltpu.VMEM(far_ut.shape, F32),
            pltpu.VMEM(far_vt.shape, F32),
            pltpu.VMEM((chunks, width, block), F32),
            pltpu.VMEM((chunks, n_dir - 1, width, block), F32),
            pltpu.VMEM((chunks, n_col, width, block), F32),
            pltpu.VMEM((n_col, 2 * width, 2 * block), BF16),
            pltpu.VMEM((n_near + n_far, width, block), F32),
            pltpu.VMEM((depth, n_dir * n_row, width, piece), F32),
            pltpu.VMEM((chunks, n_dir - 1, n_row, width, piece), F32),
            pltpu.VMEM((chunks, n_row, width, piece), F32),
            pltpu.VMEM((chunks, n_row, width, piece), F32),
            dma((2,)),
            dma((2,)),
            dma((chunks, n_dir - 1)),
            dma((chunks, n_dir - 1)),
            dma((chunks, n_x - 1)),
            dma((chunks, n_x - 1)),
            dma((chunks, n_x)),
            dma((chunks, n_x)),
            dma((chunks, n_dir - 1, n_row)),
            dma((chunks, n_dir - 1, n_row)),
            dma((chunks, n_row)),
            dma((chunks, n_row)),
        ],
        compiler_params=pltpu.CompilerParams(
            collective_id=0, has_side_effects=True, vmem_limit_bytes=67043328
        ),
    )(near_pairs, far_pairs, far_ranks, block_counts, cot, radiation, near_z, far_ut, far_vt)
    return result.reshape(chunks, 2, width // 2, piece).transpose(3, 1, 0, 2).reshape(piece, wide)


def solution(mesh):
    return jax.shard_map(
        shards,
        mesh=mesh,
        in_specs=(
            P("dir", None),
            P(None, ("row", "col"), "dir"),
            P(None, ("dir", "row", "col"), None, None),
            P(("dir", "row", "col"), None),
            P(None, ("dir", "row", "col"), None, None),
            P(None, ("dir", "row", "col"), None, None),
            P(("dir", "row", "col"), None),
            P(("dir", "row", "col")),
            P(("dir", "row", "col"), None),
        ),
        out_specs=P(("col", "dir", "row"), None),
        check_vma=False,
    )
```

time: 335 us -> 114 us (0.34)
  waiting for transfers between devices: 271 us -> 0 us
  Pallas kernels: 0 us -> 108 us
  matrix products: 29.9 us -> 0 us
  between operations: 13.2 us -> 0.03 us
  loops' own time: 7.19 us -> 0 us
  other arithmetic: 7.13 us -> 0 us
    reduce_scatter x1 -> x0, waiting for transfers between devices: 193 us -> none  [shards(): lax.psum_scatter(partial_out, ('dir', 'row'), scatter_dimension=0, tiled=...]
    pallas_call x0 -> x1, Pallas kernels: none -> 108 us  [shards(): pl.pallas_call(functools.partial(kernel, n_dir, n_row, n_col, depth), out...]
    psum x1 -> x0, waiting for transfers between devices: 42.9 us -> none  [shards(): summed = lax.psum(partial_rhs, 'dir')]
    all_gather x1 -> x0, waiting for transfers between devices: 35.3 us -> none  [shards(): shard_rhs = lax.all_gather(summed, 'col', axis=0, tiled=True)]
    dot_general x10 -> x0, matrix products: 29.9 us -> none  [the longest x6 21.8 us: transposed_dot(): lax.dot_general(left, right, (((0,), (0,)), ((), ())), precision=lax.Prec...]
    another operation x2 -> x0, loops' own time: 7.19 us -> none  [the longest x1 4.62 us: shards(): partial_out = lax.fori_loop(0, block_counts[0, 0], near_step, partial_out)]
    neg x3 -> x0, other arithmetic: 3.93 us -> none  [swap_parts(): -values[:, half_width:]]
  transfers between devices with their start and end apart: 3 -> 0, of which waited for: 3 -> 0; matrix products, arithmetic and copies ran while one was open for 0% -> 0% of each run, Pallas kernels for 0% -> 0%
where the time goes in v1:
time: 114 us
  Pallas kernels  108 us (95%)
  local copies, waits for them, and re-layouts  6.01 us (5%)
    pallas_call x1, Pallas kernels, shards(): pl.pallas_call(functools.partial(kernel, n_dir, n_row, n_col, depth), out...  108 us
    unnamed x7, local copies, waits for them, and re-layouts  2.84 us

profile of v1, /device:TPU:0, one launch (start us, length us, event | category | flops | bytes accessed | tf_op | source)
XLA Modules:
  0.0 114.0 jit_solution(11918760160769613095)
XLA Ops:
  0.0 0.0 copy-start
  0.0 0.0 copy-start.1
  0.0 1.5 %copy.14 = bf16[1024,512]{0,1:T(8,128)(2,1)S(1)} copy(bf16[1024,512]{1,0:T(8,128)(2,1)} %param.9) | data formatting | bytes 2097152 | tf_op args[0]
  1.5 1.1 copy.15
  2.6 0.0 copy-done
  2.6 0.7 copy.16.near_pairs
  3.3 0.0 copy-done.1
  3.3 0.6 copy.17.far_pairs
  3.9 108.0 %shard_map.91 = f32[4,128,256]{2,1,0:T(8,128)} custom-call(s32[8,2]{1,0:T(8,128)} %copy.16.near_pairs, s32[4,2]{1,0:T(4,128)} %copy.17.far_pairs, s32[4]{0:T(128)} %far_ranks.1, s32[1,2]{1,0:T(1,128)} %counts.1, bf16[4,128,1024]{2,1,0:T(8,128)(2,1)} %bitcast.11, bf16[2,512,1024]{2,1,0:T(8,128)(2,1)} %rad.1, f32[2,8,512,512]{3,2,1,0:T(8,128)} %near_z.1, ...), custom_call_target="tpu_custom_call" | custom-call | tf_op jit(solution)/shard_map/pallas_call | solution.py:309
  112.0 1.1 copy.18
  113.0 1.0 copy.19
Async XLA Ops:
  0.0 2.6 %copy-start = (s32[8,2]{0,1:T(2,128)S(1)}, s32[8,2]{0,1:T(2,128)}, u32[]{:S(2)}) copy-start(s32[8,2]{0,1:T(2,128)} %param.12) | copy-start | bytes 196
  0.0 3.3 %copy-start.1 = (s32[4,2]{0,1:T(2,128)S(1)}, s32[4,2]{0,1:T(2,128)}, u32[]{:S(2)}) copy-start(s32[4,2]{0,1:T(2,128)} %param.15) | copy-start | bytes 100

commit v2 on v1

--- a/solution.py
+++ b/solution.py
@@ -42,10 +42,13 @@
     n_dir, n_row, n_col, depth,
     near_pairs, far_pairs, far_ranks, counts, cot, rad, near_z, far_ut, far_vt,
     out,
-    z_high, z_low, stage, ut, vt, sent, dir_in, gathered, sides, terms, parts, dir_parts, sums, row_parts,
+    z_high, z_low, stage, far_stage, left_far, right_far, cot_t, totals, sent, dir_in, gathered, sides, terms, parts, dir_parts, sums, row_parts,
     stage_sem, far_sem, d_send, d_recv, x_send, x_recv, c_send, c_recv, p_send, p_recv, r_send, r_recv,
 ):
-    chunks, width = cot.shape[0], cot.shape[1]
+    chunks, width = sent.shape[0], sent.shape[1]
+    half = width // 2
+    wide = cot.shape[1]
+    rank_most, rank_pad = far_ut.shape[2], left_far.shape[2] // 2
     n_near, n_far = near_z.shape[1], far_ut.shape[1]
     block = near_z.shape[2]
     piece = block // n_dir
@@ -82,12 +85,17 @@
 
     load_item(0).start()
     load_item(1).start()
-    far_loads = [
-        pltpu.make_async_copy(far_ut, ut, far_sem.at[0]),
-        pltpu.make_async_copy(far_vt, vt, far_sem.at[1]),
-    ]
-    for load in far_loads:
-        load.start()
+    def load_far(s):
+        side = lax.rem(s, 2)
+        return [
+            pltpu.make_async_copy(source.at[part, s], far_stage.at[side, 2 * i + part], far_sem.at[side, 2 * i + part])
+            for i, source in enumerate((far_ut, far_vt))
+            for part in range(2)
+        ]
+
+    for s in range(min(2, n_far)):
+        for load in load_far(s):
+            load.start()
 
     peers = [dir_peer(j) for j in range(1, n_dir)]
     peers += [x_peer(j) for j in range(1, n_x)]
@@ -126,7 +134,9 @@
         )
 
     def right_sides(k):
-        left = cot[k]
+        left = jnp.concatenate(
+            [cot_t[k * half : (k + 1) * half], cot_t[wide // 2 + k * half : wide // 2 + (k + 1) * half]], axis=0
+        )
         sent[k] = dot_nt(left, rad[0]) + dot_nt(swap_rows(left), rad[1])
         for j in range(1, n_dir):
             send_dir(k, j).start()
@@ -146,6 +156,34 @@
             return carry
 
         lax.fori_loop(2 * first, 2 * last, body, 0)
+
+    def pack_far():
+        rest = jnp.zeros((rank_pad - rank_most, block), F32)
+
+        def body(s, carry):
+            for load in load_far(s):
+                load.wait()
+            side = lax.rem(s, 2)
+            for part in range(2):
+                factor = jnp.concatenate([far_stage[side, part], rest], axis=0)
+                high, low = split(factor.T)
+                rows = slice(part * block, (part + 1) * block)
+                left_far[s, rows, :rank_pad] = high
+                left_far[s, rows, rank_pad:] = low
+                factor = jnp.concatenate([far_stage[side, 2 + part], rest], axis=0)
+                high, low = split(factor)
+                rows = slice(part * rank_pad, (part + 1) * rank_pad)
+                right_far[0, s, rows, :] = high
+                right_far[1, s, rows, :] = low
+
+            @pl.when(s + 2 < n_far)
+            def _():
+                for load in load_far(s + 2):
+                    load.start()
+
+            return carry
+
+        lax.fori_loop(0, n_far, body, 0)
 
     def add_dirs(k):
         for j in range(1, n_dir):
@@ -188,17 +226,13 @@
 
         def far(s, carry):
             left = sides[lax.rem(far_pairs[s, 0], n_col)]
-            high, low = split(jnp.concatenate([ut[0, s], ut[1, s]], axis=1))
-            coeffs = fold(dot_nt(left, high)) + dot_nt(left[:width], low)
+            both = dot(left, left_far[s])
+            coeffs = fold(both[:, :rank_pad]) + both[:width, rank_pad:]
             lanes = lax.broadcasted_iota(jnp.int32, coeffs.shape, 1)
             coeffs = jnp.where(lanes < far_ranks[s], coeffs, 0.0)
-            c_high, c_low = split(coeffs)
-            s_high, s_low = split(swap_rows(coeffs))
-            re_high, re_low = split(vt[0, s])
-            im_high, im_low = split(vt[1, s])
-            both = dot(jnp.concatenate([c_high, c_low], axis=0), re_high)
-            both = both + dot(jnp.concatenate([s_high, s_low], axis=0), im_high)
-            terms[n_near + s] = fold(both) + (dot(c_high, re_low) + dot(s_high, im_low))
+            high, low = split(jnp.concatenate([coeffs, swap_rows(coeffs)], axis=1))
+            both = dot(jnp.concatenate([high, low], axis=0), right_far[0, s])
+            terms[n_near + s] = fold(both) + dot(high, right_far[1, s])
             return carry
 
         lax.fori_loop(0, n_far, far, 0)
@@ -245,8 +279,15 @@
                 sums.at[k, src], row_parts.at[k, src], r_send.at[k, src], r_recv.at[k, src], row_peer(i)
             ).wait_recv()
             total = total + row_parts[k, src]
-        out[k] = total
-
+        totals[k * half : (k + 1) * half] = total[:half]
+        totals[wide // 2 + k * half : wide // 2 + (k + 1) * half] = total[half:]
+        if k % group == group - 1:
+            for base in (0, wide // 2):
+                columns = slice(base + (k + 1 - group) * half, base + (k + 1) * half)
+                out[:, columns] = totals[columns].T
+
+    group = max(1, 128 // half)
+    cot_t[...] = cot[...].T
     for k in range(chunks):
         right_sides(k)
     steps = chunks
@@ -257,8 +298,7 @@
             add_dirs(i)
         if i >= 1:
             relay(i - 1)
-    for load in far_loads:
-        load.wait()
+    pack_far()
     products(0)
     add_dirs(chunks - 1)
     for k in range(1, chunks):
@@ -301,22 +341,25 @@
     n_x = n_col // CORES
     piece = block // n_dir
     depth = chunks if n_row * n_col <= 16 else 2
-    cot = cotangent.T.reshape(2, chunks, width // 2, deep).transpose(1, 0, 2, 3).reshape(chunks, width, deep)
+    rank_pad = -(-rank_most // 128) * 128
     vmem = pl.BlockSpec(memory_space=pltpu.VMEM)
     smem = pl.BlockSpec(memory_space=pltpu.SMEM)
     anywhere = pl.BlockSpec(memory_space=pl.ANY)
     dma = pltpu.SemaphoreType.DMA
-    result = pl.pallas_call(
+    return pl.pallas_call(
         functools.partial(kernel, n_dir, n_row, n_col, depth),
-        out_shape=jax.ShapeDtypeStruct((chunks, width, piece), F32),
+        out_shape=jax.ShapeDtypeStruct((piece, wide), F32),
         in_specs=[smem] * 4 + [vmem] * 2 + [anywhere] * 3,
         out_specs=vmem,
         scratch_shapes=[
             pltpu.VMEM((n_near, 2 * block, block), BF16),
             pltpu.VMEM((n_near, 2 * block, block), BF16),
             pltpu.VMEM((2, block, block), F32),
-            pltpu.VMEM(far_ut.shape, F32),
-            pltpu.VMEM(far_vt.shape, F32),
+            pltpu.VMEM((2, 4, rank_most, block), F32),
+            pltpu.VMEM((n_far, 2 * block, 2 * rank_pad), BF16),
+            pltpu.VMEM((2, n_far, 2 * rank_pad, block), BF16),
+            pltpu.VMEM((wide, deep), BF16),
+            pltpu.VMEM((wide, piece), F32),
             pltpu.VMEM((chunks, width, block), F32),
             pltpu.VMEM((chunks, n_dir - 1, width, block), F32),
             pltpu.VMEM((chunks, n_col, width, block), F32),
@@ -327,7 +370,7 @@
             pltpu.VMEM((chunks, n_row, width, piece), F32),
             pltpu.VMEM((chunks, n_row, width, piece), F32),
             dma((2,)),
-            dma((2,)),
+            dma((2, 4)),
             dma((chunks, n_dir - 1)),
             dma((chunks, n_dir - 1)),
             dma((chunks, n_x - 1)),
@@ -342,8 +385,7 @@
         compiler_params=pltpu.CompilerParams(
             collective_id=0, has_side_effects=True, vmem_limit_bytes=67043328
         ),
-    )(near_pairs, far_pairs, far_ranks, block_counts, cot, radiation, near_z, far_ut, far_vt)
-    return result.reshape(chunks, 2, width // 2, piece).transpose(3, 1, 0, 2).reshape(piece, wide)
+    )(near_pairs, far_pairs, far_ranks, block_counts, cotangent, radiation, near_z, far_ut, far_vt)
 
 
 def solution(mesh):

time: 114 us -> 111 us (0.974)
  Pallas kernels: 108 us -> 106 us
  local copies, waits for them, and re-layouts: 6.01 us -> 4.56 us
    reshape x2 -> x0, local copies, waits for them, and re-layouts: 2.08 us -> none  [shards(): result.reshape(chunks, 2, width // 2, piece).transpose(3, 1, 0, 2)]
    pallas_call x1, Pallas kernels: 108 us -> 106 us  [shards(): pl.pallas_call(functools.partial(kernel, n_dir, n_row, n_col, depth), out...]
    unnamed x7 -> x3, local copies, waits for them, and re-layouts: 2.84 us -> 4.56 us
where the time goes in v2:
time: 111 us
  Pallas kernels  106 us (95%)
  local copies, waits for them, and re-layouts  4.56 us (4%)
    pallas_call x1, Pallas kernels, shards(): pl.pallas_call(functools.partial(kernel, n_dir, n_row, n_col, depth), out...  106 us
    unnamed x3, local copies, waits for them, and re-layouts  4.56 us

profile of v2, /device:TPU:0, one launch (start us, length us, event | category | flops | bytes accessed | tf_op | source)
XLA Modules:
  0.0 110.8 jit_solution(7705741730880483725)
XLA Ops:
  0.0 1.4 %copy.11.far_pairs = s32[4,2]{1,0:T(4,128)} copy(s32[4,2]{0,1:T(2,128)} %param.15) | data formatting | bytes 64 | tf_op args[6]
  1.4 1.3 %copy.10.near_pairs = s32[8,2]{1,0:T(8,128)} copy(s32[8,2]{0,1:T(2,128)} %param.12) | data formatting | bytes 128 | tf_op args[3]
  2.7 106.2 %shard_map.91 = f32[256,512]{1,0:T(8,128)} custom-call(s32[8,2]{1,0:T(8,128)} %copy.10.near_pairs, s32[4,2]{1,0:T(4,128)} %copy.11.far_pairs, s32[4]{0:T(128)} %far_ranks.1, s32[1,2]{1,0:T(1,128)} %counts.1, bf16[1024,512]{1,0:T(8,128)(2,1)} %cot.1, bf16[2,512,1024]{2,1,0:T(8,128)(2,1)} %rad.1, f32[2,8,512,512]{3,2,1,0:T(8,128)} %near_z.1, ...), custom_call_target="tpu_custom_call" | custom-call | tf_op jit(solution)/shard_map/pallas_call | solution.py:349
  108.9 1.9 %copy.13 = f32[256,512]{1,0:T(8,128)} copy(f32[256,512]{1,0:T(8,128)} %shard_map.91) | data formatting | bytes 1048576

commit v3 on v2

--- a/solution.py
+++ b/solution.py
@@ -48,6 +48,7 @@
     chunks, width = sent.shape[0], sent.shape[1]
     half = width // 2
     wide = cot.shape[1]
+    stages = stage.shape[0]
     rank_most, rank_pad = far_ut.shape[2], left_far.shape[2] // 2
     n_near, n_far = near_z.shape[1], far_ut.shape[1]
     block = near_z.shape[2]
@@ -80,11 +81,11 @@
     def load_item(item):
         slot, part = item // 2, lax.rem(item, 2)
         return pltpu.make_async_copy(
-            near_z.at[part, slot], stage.at[lax.rem(item, 2)], stage_sem.at[lax.rem(item, 2)]
-        )
-
-    load_item(0).start()
-    load_item(1).start()
+            near_z.at[part, slot], stage.at[lax.rem(item, stages)], stage_sem.at[lax.rem(item, stages)]
+        )
+
+    for item in range(stages):
+        load_item(item).start()
     def load_far(s):
         side = lax.rem(s, 2)
         return [
@@ -144,14 +145,14 @@
     def convert(first, last):
         def body(item, carry):
             load_item(item).wait()
-            high, low = split(stage[lax.rem(item, 2)])
+            high, low = split(stage[lax.rem(item, stages)])
             rows = pl.ds(pl.multiple_of(lax.rem(item, 2) * block, block), block)
             z_high[item // 2, rows, :] = high
             z_low[item // 2, rows, :] = low
 
-            @pl.when(item + 2 < 2 * n_near)
+            @pl.when(item + stages < 2 * n_near)
             def _():
-                load_item(item + 2).start()
+                load_item(item + stages).start()
 
             return carry
 
@@ -217,25 +218,26 @@
 
         lax.fori_loop(0, n_col, side, 0)
 
-        def near(s, carry):
+        per_far = n_near // n_far
+
+        def near(s):
             left = sides[lax.rem(near_pairs[s, 0], n_col)]
             terms[s] = fold(dot(left, z_high[s])) + dot(left[:width], z_low[s])
-            return carry
-
-        lax.fori_loop(0, n_near, near, 0)
-
-        def far(s, carry):
-            left = sides[lax.rem(far_pairs[s, 0], n_col)]
-            both = dot(left, left_far[s])
+
+        def body(s, carry):
+            both = dot(sides[lax.rem(far_pairs[s, 0], n_col)], left_far[s])
+            near(s * per_far)
             coeffs = fold(both[:, :rank_pad]) + both[:width, rank_pad:]
             lanes = lax.broadcasted_iota(jnp.int32, coeffs.shape, 1)
             coeffs = jnp.where(lanes < far_ranks[s], coeffs, 0.0)
             high, low = split(jnp.concatenate([coeffs, swap_rows(coeffs)], axis=1))
+            for i in range(1, per_far):
+                near(s * per_far + i)
             both = dot(jnp.concatenate([high, low], axis=0), right_far[0, s])
             terms[n_near + s] = fold(both) + dot(high, right_far[1, s])
             return carry
 
-        lax.fori_loop(0, n_far, far, 0)
+        lax.fori_loop(0, n_far, body, 0)
 
         if k >= depth:
             for j in range(1, n_dir):
@@ -340,7 +342,9 @@
     n_near, n_far, rank_most = near_z.shape[1], far_ut.shape[1], far_ut.shape[2]
     n_x = n_col // CORES
     piece = block // n_dir
-    depth = chunks if n_row * n_col <= 16 else 2
+    small = n_row * n_col <= 16
+    depth = chunks if small else 2
+    stages = min(6 if small else 2, 2 * n_near)
     rank_pad = -(-rank_most // 128) * 128
     vmem = pl.BlockSpec(memory_space=pltpu.VMEM)
     smem = pl.BlockSpec(memory_space=pltpu.SMEM)
@@ -354,7 +358,7 @@
         scratch_shapes=[
             pltpu.VMEM((n_near, 2 * block, block), BF16),
             pltpu.VMEM((n_near, 2 * block, block), BF16),
-            pltpu.VMEM((2, block, block), F32),
+            pltpu.VMEM((stages, block, block), F32),
             pltpu.VMEM((2, 4, rank_most, block), F32),
             pltpu.VMEM((n_far, 2 * block, 2 * rank_pad), BF16),
             pltpu.VMEM((2, n_far, 2 * rank_pad, block), BF16),
@@ -369,7 +373,7 @@
             pltpu.VMEM((chunks, n_dir - 1, n_row, width, piece), F32),
             pltpu.VMEM((chunks, n_row, width, piece), F32),
             pltpu.VMEM((chunks, n_row, width, piece), F32),
-            dma((2,)),
+            dma((stages,)),
             dma((2, 4)),
             dma((chunks, n_dir - 1)),
             dma((chunks, n_dir - 1)),

time: 111 us -> 104 us (0.937)
  Pallas kernels: 106 us -> 99.1 us
    pallas_call x1, Pallas kernels: 106 us -> 99.1 us  [shards(): pl.pallas_call(functools.partial(kernel, n_dir, n_row, n_col, depth), out...]
where the time goes in v3:
time: 104 us
  Pallas kernels  99.1 us (95%)
  local copies, waits for them, and re-layouts  4.56 us (4%)
    pallas_call x1, Pallas kernels, shards(): pl.pallas_call(functools.partial(kernel, n_dir, n_row, n_col, depth), out...  99.1 us
    unnamed x3, local copies, waits for them, and re-layouts  4.56 us

profile of v3, /device:TPU:0, one launch (start us, length us, event | category | flops | bytes accessed | tf_op | source)
XLA Modules:
  0.0 103.7 jit_solution(14015752977729101451)
XLA Ops:
  0.0 1.4 %copy.11.far_pairs = s32[4,2]{1,0:T(4,128)} copy(s32[4,2]{0,1:T(2,128)} %param.15) | data formatting | bytes 64 | tf_op args[6]
  1.4 1.3 %copy.10.near_pairs = s32[8,2]{1,0:T(8,128)} copy(s32[8,2]{0,1:T(2,128)} %param.12) | data formatting | bytes 128 | tf_op args[3]
  2.7 99.1 %shard_map.91 = f32[256,512]{1,0:T(8,128)} custom-call(s32[8,2]{1,0:T(8,128)} %copy.10.near_pairs, s32[4,2]{1,0:T(4,128)} %copy.11.far_pairs, s32[4]{0:T(128)} %far_ranks.1, s32[1,2]{1,0:T(1,128)} %counts.1, bf16[1024,512]{1,0:T(8,128)(2,1)} %cot.1, bf16[2,512,1024]{2,1,0:T(8,128)(2,1)} %rad.1, f32[2,8,512,512]{3,2,1,0:T(8,128)} %near_z.1, ...), custom_call_target="tpu_custom_call" | custom-call | tf_op jit(solution)/shard_map/pallas_call | solution.py:353
  101.8 1.9 %copy.13 = f32[256,512]{1,0:T(8,128)} copy(f32[256,512]{1,0:T(8,128)} %shard_map.91) | data formatting | bytes 1048576
